TPU v7x, 32 devices: a whole 2x2x4 slice. The times are simulated.
32 devices in a mesh: grp: 2 (over y), ctx: 4 (over x, core), head: 4 (over z).
Axes of the slice: x: 2, y: 2, z: 4, core: 2. Of those that a mesh axis runs over, the one named last changes fastest.
Arguments:
- prompt_hidden: bfloat16 [4, 1024, 4096], P('grp', 'ctx', 'head'), parts along dimension 0, may hold values from -3 to 3
- qkv_weight: bfloat16 [3, 4096, 4096], P(None, 'ctx', 'head'), may hold values from -0.09375 to 0.09375
- out_weight: bfloat16 [4096, 4096], P('head', 'ctx'), may hold values from -0.9375 to 0.9375
- embed_table: bfloat16 [32768, 4096], P('ctx', 'head'), may hold values from -60 to 60
- response_ids: int32 [4, 256], P(None, 'grp'), parts along dimension 1, may hold values from 0 to 32767
- assignment: int32 [256], P('grp'), parts along dimension 0, may hold values from 0 to 1
Outputs:
- final_hidden: bfloat16 [4, 256, 4096], P(None, ('grp', 'ctx'), 'head'), parts along dimension 1
There are 2 independent parts, one for each index of `grp`. A program takes and returns all parts, laid end to end along the dimension named above; an argument that names none is the same for every part. Nothing has to cross between parts.
All inputs are finite; a program needn't handle non-finite values.
Results may differ from a plain program's by a relative error of at most 0.023.
Values may be sent and summed in bfloat16 or wider, within the bound.
A program may use at most 128 MiB of HBM per device.

v0:
```python
import jax
import jax.numpy as jnp
from jax import lax
from jax.sharding import PartitionSpec as P

DH = 128


def rms_rows(values):
    return values * lax.rsqrt(jnp.mean(values * values, axis=-1, keepdims=True) + 1e-06)


def on_device(prompt_hidden, qkv_weight, out_weight, embed_table, response_ids, assignment):
    local_cols = prompt_hidden.shape[2]
    prompt_rows = prompt_hidden.shape[1]
    head_size = DH
    local_heads = local_cols // head_size
    steps = response_ids.shape[0]
    resp_local = response_ids.shape[1] // lax.axis_size("ctx")
    ctx_index = lax.axis_index("ctx")
    full_rows = lax.all_gather(qkv_weight, "ctx", axis=1, tiled=True)
    kv_weight = jnp.concatenate([full_rows[1], full_rows[2]], axis=1)
    piece = lax.all_gather(prompt_hidden, "head", axis=2, tiled=True)
    flat_piece = piece.reshape(2 * prompt_rows, piece.shape[2])
    kv_local = jnp.dot(flat_piece, kv_weight, preferred_element_type=jnp.float32)
    kv_local = kv_local.astype(jnp.bfloat16).reshape(2, prompt_rows, 2, local_heads, head_size)
    partial_state = jnp.einsum(
        "pthd,pthe->phde", kv_local[:, :, 0], kv_local[:, :, 1], preferred_element_type=jnp.float32
    )
    state = lax.psum(partial_state.astype(jnp.bfloat16), "ctx").astype(jnp.float32)
    vocab_rows = embed_table.shape[0]
    offset_ids = response_ids - ctx_index * vocab_rows
    inside = (offset_ids >= 0) & (offset_ids < vocab_rows)
    looked = jnp.take(embed_table, jnp.clip(offset_ids, 0, vocab_rows - 1), axis=0)
    looked = jnp.where(inside[:, :, None], looked.astype(jnp.float32), 0.0)
    embedded_mine = lax.psum_scatter(
        looked.astype(jnp.bfloat16), "ctx", scatter_dimension=1, tiled=True
    )
    embedded = lax.all_gather(embedded_mine, "head", axis=2, tiled=True)
    normed = rms_rows(embedded.astype(jnp.float32)).astype(jnp.bfloat16)
    projected_qkv = jnp.einsum(
        "trd,kde->trke", normed, full_rows, preferred_element_type=jnp.float32
    ).astype(jnp.bfloat16)
    projected_qkv = projected_qkv.reshape(steps, resp_local, 3, local_heads, head_size)
    query = projected_qkv[:, :, 0]
    key = projected_qkv[:, :, 1]
    value = projected_qkv[:, :, 2]
    my_prompt = lax.dynamic_slice_in_dim(assignment, ctx_index * resp_local, resp_local, 0)
    query_f = query.astype(jnp.float32)
    both = jnp.einsum("trhd,phde->ptrhe", query_f, state, precision=lax.Precision.HIGHEST)
    chosen = jnp.where((my_prompt == 0)[None, :, None, None], both[0], both[1])
    scores = jnp.einsum("trhd,srhd->rhts", query, key, preferred_element_type=jnp.float32)
    later = jnp.arange(steps)[:, None] >= jnp.arange(steps)[None, :]
    scores = jnp.where(later[None, None], scores, 0.0).astype(jnp.bfloat16)
    local = jnp.einsum("rhts,srhd->trhd", scores, value, preferred_element_type=jnp.float32)
    head_out = rms_rows(chosen + local).astype(jnp.bfloat16).reshape(steps, resp_local, local_cols)
    terms = jnp.einsum(
        "trd,de->tre",
        head_out,
        lax.all_gather(out_weight, "ctx", axis=1, tiled=True),
        preferred_element_type=jnp.float32,
    )
    width = terms.shape[2]
    mine = lax.psum_scatter(
        terms.astype(jnp.bfloat16), "head", scatter_dimension=2, tiled=True
    ).astype(jnp.float32)
    mixed = embedded_mine.astype(jnp.float32) + mine
    squares = lax.psum(jnp.sum(mixed * mixed, axis=-1), "head")
    result = mixed * lax.rsqrt(squares[:, :, None] / width + 1e-06)
    return result.astype(jnp.bfloat16)


def solution(mesh):
    return jax.shard_map(
        on_device,
        mesh=mesh,
        in_specs=(
            P("grp", "ctx", "head"),
            P(None, "ctx", "head"),
            P("head", "ctx"),
            P("ctx", "head"),
            P(None, "grp"),
            P("grp"),
        ),
        out_specs=P(None, ("grp", "ctx"), "head"),
        check_vma=False,
    )
```

profile of v0, /device:TPU:0, one launch (start us, length us, event | category | flops | bytes accessed | tf_op | source)
XLA Modules:
  0.0 461.3 jit_solution(4606842393122182999)
XLA Ops:
  6.5 0.7 compare_and_fusion.1
  7.9 10.7 %gather_fusion = bf16[512,1024]{1,0:T(8,128)(2,1)S(1)} fusion(bf16[8192,1024]{1,0:T(8,128)(2,1)} %param.9, s32[1024]{0:T(1024)S(1)} %pad_clamp_fusion), kind=kCustom, calls=%fused_computation | custom fusion | bytes 2099200 | tf_op jit(solution)/shard_map/jit(_take)/gather | solution.py:34
  18.6 1.4 select_convert_fusion
  20.0 0.7 all-gather.5.cloned.1.call-update
  21.5 26.1 %reduce-scatter.3.cloned.1.call-done = bf16[4,32,1024]{2,1,0:T(8,128)(2,1)} async-done(((bf16[4,128,1024]{2,1,0:T(8,128)(2,1)}), bf16[4,32,1024]{2,1,0:T(8,128)(2,1)}) %reduce-scatter.3.cloned.1.call-update) | async-done | bytes 262160 | tf_op jit(solution)/shard_map/reduce_scatter | solution.py:36
  47.9 156.1 %all-gather.5.cloned.1.call-done = bf16[3,4096,1024]{2,1,0:T(8,128)(2,1)} async-done(((bf16[3,1024,1024]{2,1,0:T(8,128)(2,1)}), bf16[3,4096,1024]{2,1,0:T(8,128)(2,1)}) %all-gather.5.cloned.1.call-update) | async-done | bytes 25165840 | tf_op jit(solution)/shard_map/all_gather | solution.py:21
  204.0 11.8 %slice_bitcast_fusion.1 = (bf16[4096,1024]{1,0:T(8,128)(2,1)}, bf16[4096,1024]{1,0:T(8,128)(2,1)}) fusion(bf16[3,4096,1024]{2,1,0:T(8,128)(2,1)} %all-gather.5.cloned.1.call-done), kind=kLoop, calls=%fused_computation.8 | loop fusion | bytes 33554432 | tf_op jit(solution)/shard_map/squeeze | solution.py:22
  215.9 70.5 %all-gather.7.cloned.1.call-done = bf16[2,256,4096]{2,1,0:T(8,128)(2,1)} async-done(((bf16[2,256,1024]{2,1,0:T(8,128)(2,1)}), bf16[2,256,4096]{2,1,0:T(8,128)(2,1)}) %all-gather.7.cloned.1.call-update) | async-done | bytes 4194320 | tf_op jit(solution)/shard_map/all_gather | solution.py:23
  286.4 17.3 %fusion.14 = bf16[512,2048]{0,1:T(8,128)(2,1)} fusion(bf16[512,4096]{1,0:T(8,128)(2,1)} %bitcast.86, bf16[4096,1024]{1,0:T(8,128)(2,1)} %get-tuple-element.8, bf16[4096,1024]{1,0:T(8,128)(2,1)} %get-tuple-element.7), kind=kOutput, calls=%fused_computation.13 | convolution fusion | flops 8624537600 | bytes 23068672 | tf_op jit(solution)/shard_map/dot_general | solution.py:25
  303.7 2.6 reshape.52
  306.3 1.5 slice_bitcast_fusion.3
  307.8 1.3 convolution_convert_fusion
  310.0 4.3 all-gather.9.cloned.1.call-done
  314.3 1.5 fusion.17
  315.9 12.1 %fusion.19 = bf16[4,32,3,1024]{3,1,2,0:T(8,128)(2,1)S(1)} fusion(bf16[3,4096,1024]{2,1,0:T(8,128)(2,1)} %all-gather.5.cloned.1.call-done, bf16[4,32,4096]{2,1,0:T(8,128)(2,1)} %all-gather.9.cloned.1.call-done, f32[4,32]{1,0:T(4,128)S(1)} %add_rsqrt_fusion.2), kind=kOutput, calls=%fused_computation.19 | convolution fusion | flops 3223191552 | bytes 27001344 | tf_op jit(solution)/shard_map/trd,kde->trke/dot_general | solution.py:41
  328.3 0.7 fusion.23
  329.0 20.3 %all-reduce.2.cloned.1.call-done = bf16[2,8,128,128]{3,2,0,1:T(8,128)(2,1)} async-done(((bf16[2,8,128,128]{3,2,0,1:T(8,128)(2,1)}), bf16[2,8,128,128]{3,2,0,1:T(8,128)(2,1)}) %all-reduce.2.cloned.1.call-update) | async-done | bytes 524304 | tf_op jit(solution)/shard_map/psum | solution.py:30
  349.3 1.3 convolution_bitcast_fusion
  351.1 58.0 %all-gather.11.cloned.1.call-done = bf16[1024,4096]{1,0:T(8,128)(2,1)} async-done(((bf16[1024,1024]{1,0:T(8,128)(2,1)}), bf16[1024,4096]{1,0:T(8,128)(2,1)}) %all-gather.11.cloned.1.call-update) | async-done | bytes 8388624 | tf_op jit(solution)/shard_map/all_gather | solution.py:60
  409.2 5.7 %fusion.8 = bf16[4,32,4096]{2,1,0:T(8,128)(2,1)} fusion(bf16[1024,4096]{1,0:T(8,128)(2,1)} %all-gather.11.cloned.1.call-done, f32[4,32,8,128]{3,1,0,2:T(8,128)S(1)} %get-tuple-element.6, f32[4,32,8]{1,0,2:T(4,128)S(1)} %add_rsqrt_fusion), kind=kOutput, calls=%fused_computation.11 | convolution fusion | flops 1074528256 | bytes 9965568 | tf_op jit(solution)/shard_map/trd,de->tre/dot_general | solution.py:57
  414.9 27.4 %reduce-scatter.5.cloned.1.call-done = bf16[4,32,1024]{2,1,0:T(8,128)(2,1)} async-done(((bf16[4,32,4096]{2,1,0:T(8,128)(2,1)}), bf16[4,32,1024]{2,1,0:T(8,128)(2,1)}) %reduce-scatter.5.cloned.1.call-update) | async-done | bytes 262160 | tf_op jit(solution)/shard_map/reduce_scatter | solution.py:64
  442.3 1.1 multiply_reduce_fusion
  443.4 9.3 %psum.15 = f32[4,32]{1,0:T(4,128)S(1)} all-reduce(f32[4,32]{1,0:T(4,128)S(1)} %multiply_reduce_fusion), channel_id=1, replica_groups=mesh['grp'=2,'ctx'=4,'head'=4] {'head'}, use_global_device_ids=true, to_apply=%region_6.7 | all-reduce | flops 128 | bytes 1024 | tf_op jit(solution)/shard_map/psum | solution.py:68
  452.7 1.8 multiply_convert_fusion
  (27 shorter events, 3.5 us)
Async XLA Ops:
  6.5 41.1 %reduce-scatter.3.cloned.1.call-start = ((), (), s32[]{:S(2)}) async-start(), calls=%async_computation.2 | async-start | bytes 1310720 | tf_op jit(solution)/shard_map/reduce_scatter | solution.py:36
  20.0 184.1 %all-gather.5.cloned.1.call-start = ((), (), s32[]{:S(2)}) async-start(), calls=%async_computation.3 | async-start | bytes 31457280 | tf_op jit(solution)/shard_map/all_gather | solution.py:21
  20.7 265.7 %all-gather.7.cloned.1.call-start = ((), (), s32[]{:S(2)}) async-start(), calls=%async_computation.4 | async-start | bytes 5242880 | tf_op jit(solution)/shard_map/all_gather | solution.py:23
  21.5 292.8 %all-gather.9.cloned.1.call-start = ((), (), s32[]{:S(2)}) async-start(), calls=%async_computation.6 | async-start | bytes 1310720 | tf_op jit(solution)/shard_map/all_gather | solution.py:39
  47.7 301.7 %all-reduce.2.cloned.1.call-start = ((), (), s32[]{:S(2)}) async-start(), calls=%async_computation.5 | async-start | bytes 1048576 | tf_op jit(solution)/shard_map/psum | solution.py:30
  303.7 6.2 %copy-start.1 = (s32[128]{0:T(128)S(1)}, s32[128]{0:T(128)}, u32[]{:S(2)}) copy-start(s32[128]{0:T(128)} %param.11) | copy-start | bytes 1540
  309.1 100.1 %all-gather.11.cloned.1.call-start = ((), (), s32[]{:S(2)}) async-start(), calls=%async_computation.7 | async-start | bytes 10485760 | tf_op jit(solution)/shard_map/all_gather | solution.py:60
  309.7 132.6 %reduce-scatter.5.cloned.1.call-start = ((), (), s32[]{:S(2)}) async-start(), calls=%async_computation.8 | async-start | bytes 1310720 | tf_op jit(solution)/shard_map/reduce_scatter | solution.py:64
  329.0 113.3 %copy-start = (bf16[4,32,1024]{2,1,0:T(8,128)(2,1)S(1)}, bf16[4,32,1024]{2,1,0:T(8,128)(2,1)}, u32[]{:S(2)}) copy-start(bf16[4,32,1024]{2,1,0:T(8,128)(2,1)} %reduce-scatter.3.cloned.1.call-done) | copy-start | bytes 786436
Sparse Core Ops, SparseCore 0:
  20.1 27.4 reduce-scatter.2
  49.2 154.7 all-gather.4
  205.6 80.7 all-gather.6
  287.8 26.4 all-gather.8
  316.5 32.7 all-reduce.1
  350.8 58.3 all-gather.10
  415.0 27.2 reduce-scatter.4
where the time goes:
time: 462 us; the launch traced here: 461 us
  waiting for transfers between devices  365 us (79%)
  matrix products  38.4 us (8%)
  local copies, waits for them, and re-layouts  26.9 us (6%)
  between operations  13.6 us (3%)
  blocking collectives  9.28 us (2%)
  other arithmetic  7.7 us (2%)
    all_gather x1, waiting for transfers between devices, on_device(): full_rows = lax.all_gather(qkv_weight, 'ctx', axis=1, tiled=True)  156 us
    all_gather x1, waiting for transfers between devices, on_device(): piece = lax.all_gather(prompt_hidden, 'head', axis=2, tiled=True)  70.5 us
    all_gather x1, waiting for transfers between devices, on_device(): lax.all_gather(out_weight, 'ctx', axis=1, tiled=True)  58 us
    reduce_scatter x1, waiting for transfers between devices, on_device(): lax.psum_scatter(terms.astype(jnp.bfloat16), 'head', scatter_dimension=2,...  27.4 us
    reduce_scatter x1, waiting for transfers between devices, on_device(): lax.psum_scatter(looked.astype(jnp.bfloat16), 'ctx', scatter_dimension=1,...  26.1 us
    psum x1, waiting for transfers between devices, on_device(): lax.psum(partial_state.astype(jnp.bfloat16), 'ctx').astype(jnp.float32)  20.3 us
    dot_general x1, matrix products, on_device(): jnp.dot(flat_piece, kv_weight, preferred_element_type=jnp.float32)  17.3 us
    dot_general x1, matrix products, on_device(): jnp.einsum('trd,kde->trke', normed, full_rows, preferred_element_type=jnp...  12.1 us
  transfers between devices with their start and end apart: 7, of which 7 were waited for; matrix products, arithmetic and copies ran while one was open for 11% of the time, Pallas kernels for 0%

commit v1 on v0

--- a/solution.py
+++ b/solution.py
@@ -54,12 +54,19 @@
     scores = jnp.where(later[None, None], scores, 0.0).astype(jnp.bfloat16)
     local = jnp.einsum("rhts,srhd->trhd", scores, value, preferred_element_type=jnp.float32)
     head_out = rms_rows(chosen + local).astype(jnp.bfloat16).reshape(steps, resp_local, local_cols)
-    terms = jnp.einsum(
-        "trd,de->tre",
-        head_out,
-        lax.all_gather(out_weight, "ctx", axis=1, tiled=True),
-        preferred_element_type=jnp.float32,
-    )
+    size, place, rows = (lax.axis_size("ctx"), lax.axis_index("ctx"), out_weight.shape[1])
+    right = [(i, (i + 1) % size) for i in range(size)]
+    carried, whole = (out_weight, None)
+    for lap in range(size):
+        source = (place - lap) % size
+        arriving = lax.ppermute(carried, "ctx", right) if lap < size - 1 else None
+        made = jnp.einsum("trd,de->tre", head_out, carried, preferred_element_type=jnp.float32)
+        length = made.shape[2]
+        if whole is None:
+            whole = jnp.zeros((*made.shape[:2], size * length, *made.shape[2 + 1 :]), made.dtype)
+        whole = lax.dynamic_update_slice_in_dim(whole, made, source * length, axis=2)
+        carried = arriving
+    terms = whole
     width = terms.shape[2]
     mine = lax.psum_scatter(
         terms.astype(jnp.bfloat16), "head", scatter_dimension=2, tiled=True

time: 462 us -> 455 us (0.985)
  waiting for transfers between devices: 365 us -> 355 us
    all_gather x1 -> x0, waiting for transfers between devices: 58 us -> none  [on_device(): lax.all_gather(out_weight, 'ctx', axis=1, tiled=True)]
    ppermute x0 -> x3, waiting for transfers between devices: none -> 56.8 us  [on_device(): arriving = lax.ppermute(carried, 'ctx', right) if lap < size - 1 else None]
    all_gather x1, waiting for transfers between devices: 70.5 us -> 58.4 us  [on_device(): piece = lax.all_gather(prompt_hidden, 'head', axis=2, tiled=True)]
    psum x1, waiting for transfers between devices: 20.3 us -> 30.9 us  [on_device(): lax.psum(partial_state.astype(jnp.bfloat16), 'ctx').astype(jnp.float32)]
    all_gather x1, waiting for transfers between devices: 156 us -> 150 us  [on_device(): full_rows = lax.all_gather(qkv_weight, 'ctx', axis=1, tiled=True)]
  transfers between devices with their start and end apart: 7 -> 9, of which waited for: 7 -> 8; matrix products, arithmetic and copies ran while one was open for 11% -> 12% of each run, Pallas kernels for 0% -> 0%
where the time goes in v1:
time: 455 us; the launch traced here: 454 us
  waiting for transfers between devices  355 us (78%)
  matrix products  38.9 us (9%)
  local copies, waits for them, and re-layouts  29.6 us (7%)
  between operations  13.7 us (3%)
  blocking collectives  9.28 us (2%)
  other arithmetic  7.92 us (2%)
    all_gather x1, waiting for transfers between devices, on_device(): full_rows = lax.all_gather(qkv_weight, 'ctx', axis=1, tiled=True)  150 us
    all_gather x1, waiting for transfers between devices, on_device(): piece = lax.all_gather(prompt_hidden, 'head', axis=2, tiled=True)  58.4 us
    ppermute x3, waiting for transfers between devices, on_device(): arriving = lax.ppermute(carried, 'ctx', right) if lap < size - 1 else None  56.8 us
    psum x1, waiting for transfers between devices, on_device(): lax.psum(partial_state.astype(jnp.bfloat16), 'ctx').astype(jnp.float32)  30.9 us
    reduce_scatter x1, waiting for transfers between devices, on_device(): lax.psum_scatter(looked.astype(jnp.bfloat16), 'ctx', scatter_dimension=1,...  27.6 us
    reduce_scatter x1, waiting for transfers between devices, on_device(): lax.psum_scatter(terms.astype(jnp.bfloat16), 'head', scatter_dimension=2,...  27.6 us
    dot_general x1, matrix products, on_device(): jnp.dot(flat_piece, kv_weight, preferred_element_type=jnp.float32)  17.2 us
    squeeze x1, local copies, waits for them, and re-layouts, on_device(): kv_weight = jnp.concatenate([full_rows[1], full_rows[2]], axis=1)  11.9 us
  transfers between devices with their start and end apart: 9, of which 8 were waited for; matrix products, arithmetic and copies ran while one was open for 12% of the time, Pallas kernels for 0%

profile of v1, /device:TPU:0, one launch (start us, length us, event | category | flops | bytes accessed | tf_op | source)
XLA Modules:
  0.0 454.2 jit_solution(15836116626940498797)
XLA Ops:
  7.9 10.7 %gather_fusion = bf16[512,1024]{1,0:T(8,128)(2,1)S(1)} fusion(bf16[8192,1024]{1,0:T(8,128)(2,1)} %param.9, s32[1024]{0:T(1024)S(1)} %pad_clamp_fusion), kind=kCustom, calls=%fused_computation | custom fusion | bytes 2099200 | tf_op jit(solution)/shard_map/jit(_take)/gather | solution.py:34
  18.6 1.3 select_convert_fusion
  20.0 27.6 %reduce-scatter.3.cloned.1.call-done = bf16[4,32,1024]{2,1,0:T(8,128)(2,1)} async-done(((bf16[4,128,1024]{2,1,0:T(8,128)(2,1)}), bf16[4,32,1024]{2,1,0:T(8,128)(2,1)}) %reduce-scatter.3.cloned.1.call-update) | async-done | bytes 262160 | tf_op jit(solution)/shard_map/reduce_scatter | solution.py:36
  49.3 25.5 %collective-permute-done = bf16[1024,1024]{1,0:T(8,128)(2,1)} collective-permute-done((bf16[1024,1024]{1,0:T(8,128)(2,1)S(1)}, bf16[1024,1024]{1,0:T(8,128)(2,1)}, u32[]{:S(2)}, u32[]{:S(2)}) %collective-permute-start) | collective-permute-done | bytes 2097184 | tf_op jit(solution)/shard_map/ppermute | solution.py:62
  74.9 2.3 all-gather.8.cloned.1.call-done
  77.2 1.6 fusion.12
  78.8 31.3 %collective-permute-done.1 = bf16[1024,1024]{1,0:T(8,128)(2,1)} collective-permute-done((bf16[1024,1024]{1,0:T(8,128)(2,1)}, bf16[1024,1024]{1,0:T(8,128)(2,1)}, u32[]{:S(2)}, u32[]{:S(2)}) %collective-permute-start.1) | collective-permute-done | bytes 2097184 | tf_op jit(solution)/shard_map/ppermute | solution.py:62
  110.1 150.2 %all-gather.4.cloned.1.call-done = bf16[3,4096,1024]{2,1,0:T(8,128)(2,1)} async-done(((bf16[3,1024,1024]{2,1,0:T(8,128)(2,1)}), bf16[3,4096,1024]{2,1,0:T(8,128)(2,1)}) %all-gather.4.cloned.1.call-update) | async-done | bytes 25165840 | tf_op jit(solution)/shard_map/all_gather | solution.py:21
  260.3 11.7 %fusion.22 = bf16[4,32,3,1024]{3,1,2,0:T(8,128)(2,1)S(1)} fusion(bf16[3,4096,1024]{2,1,0:T(8,128)(2,1)} %all-gather.4.cloned.1.call-done, bf16[4,32,4096]{2,1,0:T(8,128)(2,1)S(1)} %copy-done, f32[4,32]{1,0:T(4,128)S(1)} %add_rsqrt_fusion.2), kind=kOutput, calls=%fused_computation.24 | convolution fusion | flops 3223191552 | bytes 27001344 | tf_op jit(solution)/shard_map/trd,kde->trke/dot_general | solution.py:41
  272.2 11.9 %slice_bitcast_fusion.1 = (bf16[4096,1024]{1,0:T(8,128)(2,1)}, bf16[4096,1024]{1,0:T(8,128)(2,1)}) fusion(bf16[3,4096,1024]{2,1,0:T(8,128)(2,1)} %all-gather.4.cloned.1.call-done), kind=kLoop, calls=%fused_computation.8 | loop fusion | bytes 33554432 | tf_op jit(solution)/shard_map/squeeze | solution.py:22
  284.0 58.4 %all-gather.6.cloned.1.call-done = bf16[2,256,4096]{2,1,0:T(8,128)(2,1)} async-done(((bf16[2,256,1024]{2,1,0:T(8,128)(2,1)}), bf16[2,256,4096]{2,1,0:T(8,128)(2,1)}) %all-gather.6.cloned.1.call-update) | async-done | bytes 4194320 | tf_op jit(solution)/shard_map/all_gather | solution.py:23
  342.5 17.2 %fusion.9 = bf16[512,2048]{0,1:T(8,128)(2,1)} fusion(bf16[512,4096]{1,0:T(8,128)(2,1)} %bitcast.105, bf16[4096,1024]{1,0:T(8,128)(2,1)} %get-tuple-element.8, bf16[4096,1024]{1,0:T(8,128)(2,1)} %get-tuple-element.7), kind=kOutput, calls=%fused_computation.10 | convolution fusion | flops 8624537600 | bytes 23068672 | tf_op jit(solution)/shard_map/dot_general | solution.py:25
  359.7 2.5 reshape.52
  362.3 1.5 slice_bitcast_fusion.3
  363.8 1.2 convolution_convert_fusion
  366.2 30.9 %all-reduce.2.cloned.1.call-done = bf16[2,8,128,128]{3,2,0,1:T(8,128)(2,1)} async-done(((bf16[2,8,128,128]{3,2,0,1:T(8,128)(2,1)}), bf16[2,8,128,128]{3,2,0,1:T(8,128)(2,1)}) %all-reduce.2.cloned.1.call-update) | async-done | bytes 524304 | tf_op jit(solution)/shard_map/psum | solution.py:30
  397.1 1.3 convolution_bitcast_fusion
  400.4 2.0 fusion.28
  402.5 2.0 fusion.31
  404.6 2.1 fusion.34
  407.6 27.6 %reduce-scatter.5.cloned.1.call-done = bf16[4,32,1024]{2,1,0:T(8,128)(2,1)} async-done(((bf16[4,32,4096]{2,1,0:T(8,128)(2,1)}), bf16[4,32,1024]{2,1,0:T(8,128)(2,1)}) %reduce-scatter.5.cloned.1.call-update) | async-done | bytes 262160 | tf_op jit(solution)/shard_map/reduce_scatter | solution.py:71
  435.2 1.1 multiply_reduce_fusion
  436.3 9.3 %psum.15 = f32[4,32]{1,0:T(4,128)S(1)} all-reduce(f32[4,32]{1,0:T(4,128)S(1)} %multiply_reduce_fusion), channel_id=1, replica_groups=mesh['grp'=2,'ctx'=4,'head'=4] {'head'}, use_global_device_ids=true, to_apply=%region_6.7 | all-reduce | flops 128 | bytes 1024 | tf_op jit(solution)/shard_map/psum | solution.py:75
  445.6 1.8 multiply_convert_fusion
  (43 shorter events, 7.5 us)
Async XLA Ops:
  6.5 41.0 %reduce-scatter.3.cloned.1.call-start = ((), (), s32[]{:S(2)}) async-start(), calls=%async_computation.2 | async-start | bytes 1310720 | tf_op jit(solution)/shard_map/reduce_scatter | solution.py:36
  19.9 57.3 %all-gather.8.cloned.1.call-start = ((), (), s32[]{:S(2)}) async-start(), calls=%async_computation.6 | async-start | bytes 1310720 | tf_op jit(solution)/shard_map/all_gather | solution.py:39
  47.6 1.6 copy-start.3
  47.6 27.2 %copy-start.5 = (s32[128]{0:T(128)S(1)}, s32[128]{0:T(128)}, u32[]{:S(2)}) copy-start(s32[128]{0:T(128)} %param.11) | copy-start | bytes 1540
  47.6 212.6 %all-gather.4.cloned.1.call-start = ((), (), s32[]{:S(2)}) async-start(), calls=%async_computation.3 | async-start | bytes 31457280 | tf_op jit(solution)/shard_map/all_gather | solution.py:21
  48.4 294.1 %all-gather.6.cloned.1.call-start = ((), (), s32[]{:S(2)}) async-start(), calls=%async_computation.4 | async-start | bytes 5242880 | tf_op jit(solution)/shard_map/all_gather | solution.py:23
  49.2 25.6 %collective-permute-start = (bf16[1024,1024]{1,0:T(8,128)(2,1)S(1)}, bf16[1024,1024]{1,0:T(8,128)(2,1)}, u32[]{:S(2)}, u32[]{:S(2)}) collective-permute-start(bf16[1024,1024]{1,0:T(8,128)(2,1)S(1)} %copy-done.3), channel_id=1, source_target_pairs={{0,4},{4,8},{8,12},{12,0},{1,5},{5,9},{9,13},{13,1},{2,6},{6,10},{... | collective-permute-start | bytes 6291464 | tf_op jit(solution)/shard_map/ppermute | solution.py:62
  49.2 347.8 %all-reduce.2.cloned.1.call-start = ((), (), s32[]{:S(2)}) async-start(), calls=%async_computation.5 | async-start | bytes 1048576 | tf_op jit(solution)/shard_map/psum | solution.py:30
  74.8 35.3 %collective-permute-start.1 = (bf16[1024,1024]{1,0:T(8,128)(2,1)}, bf16[1024,1024]{1,0:T(8,128)(2,1)}, u32[]{:S(2)}, u32[]{:S(2)}) collective-permute-start(bf16[1024,1024]{1,0:T(8,128)(2,1)} %collective-permute-done), channel_id=1, source_target_pairs={{0,4},{4,8},{8,12},{12,0},{1,5},{5,9},{9,13},{13,1},{2,6},{6,10},{... | collective-permute-start | bytes 6291464 | tf_op jit(solution)/shard_map/ppermute | solution.py:62
  77.2 183.1 %copy-start = (bf16[4,32,4096]{2,1,0:T(8,128)(2,1)S(1)}, bf16[4,32,4096]{2,1,0:T(8,128)(2,1)}, u32[]{:S(2)}) copy-start(bf16[4,32,4096]{2,1,0:T(8,128)(2,1)} %all-gather.8.cloned.1.call-done) | copy-start | bytes 3145732
  110.1 294.4 %collective-permute-start.2 = (bf16[1024,1024]{1,0:T(8,128)(2,1)}, bf16[1024,1024]{1,0:T(8,128)(2,1)}, u32[]{:S(2)}, u32[]{:S(2)}) collective-permute-start(bf16[1024,1024]{1,0:T(8,128)(2,1)} %collective-permute-done.1), channel_id=1, source_target_pairs={{0,4},{4,8},{8,12},{12,0},{1,5},{5,9},{9,13},{13,1},{2,6},{6,10},{... | collective-permute-start | bytes 6291464 | tf_op jit(solution)/shard_map/ppermute | solution.py:62
  365.0 70.2 %reduce-scatter.5.cloned.1.call-start = ((), (), s32[]{:S(2)}) async-start(), calls=%async_computation.7 | async-start | bytes 1310720 | tf_op jit(solution)/shard_map/reduce_scatter | solution.py:71
  398.4 1.6 copy-start.4
  404.5 30.7 %copy-start.2 = (bf16[4,32,1024]{2,1,0:T(8,128)(2,1)S(1)}, bf16[4,32,1024]{2,1,0:T(8,128)(2,1)}, u32[]{:S(2)}) copy-start(bf16[4,32,1024]{2,1,0:T(8,128)(2,1)} %reduce-scatter.3.cloned.1.call-done) | copy-start | bytes 786436
  406.6 1.0 copy-start.1
Sparse Core Ops, SparseCore 0:
  20.0 27.4 reduce-scatter.2
  49.1 27.9 all-gather.7
  78.7 181.4 all-gather.3
  261.7 80.7 all-gather.5
  365.1 31.8 all-reduce.1
  407.8 27.3 reduce-scatter.4
